TPU v7x, 32 devices: a whole 2x2x4 slice. The times are simulated.
32 devices in a mesh: rec: 2 (over y), gx: 16 (over z, x, core).
Axes of the slice: x: 2, y: 2, z: 4, core: 2. Of those that a mesh axis runs over, the one named last changes fastest.
Arguments:
- velocity: float32 [4, 3, 96, 16, 128], P(None, None, ('rec', 'gx')), parts along dimension 2, may hold values from -6 to 36, as said below
- span_rim: float32 [4, 2, 96, 10, 6], P(None, None, ('rec', 'gx')), parts along dimension 2, may hold values from -6 to 36, as said below
- sketch_old: bfloat16 [3, 96, 10, 128, 256], P(None, ('rec', 'gx')), parts along dimension 1, as said below
- omega: float32 [4, 256], replicated, may hold values from -6 to 6
Outputs:
- basis: bfloat16 [3, 96, 10, 128, 256], P(None, ('rec', 'gx')), parts along dimension 1
- factor: float32 [512, 256], P('rec'), parts along dimension 0
There are 2 independent parts, one for each index of `rec`. A program takes and returns all parts, laid end to end along the dimension named above; an argument that names none is the same for every part. Nothing has to cross between parts.
Inputs may be any that keep to these rules, and one draw needn't show every extreme that they name: `sketch_old`: finite values of order one; rows differ in scale. `velocity`: finite values. `span_rim`: finite values.
All inputs are finite; a program needn't handle non-finite values.
Results may differ from a plain program's by a relative error of at most 0.014.
The roundings to bfloat16 on the way count: a program that leaves them out, or rounds other values in their place, can miss the bound.
Values sent between devices are 32-bit elements; how exact they have to be, the bound alone decides.
No kernel may reach another device: no remote copies, remote signals or barrier semaphores. Data moves between devices by JAX's collectives and lax.ppermute only.
A program may use at most 64 MiB of HBM per device.

v0:
```python
import jax
import jax.numpy as jnp
from jax import lax
from jax.sharding import PartitionSpec as P

COEFS = (0.75, -0.15, 1.0 / 60.0)


def extended_2(cells, sides, width):
    for axis, dim in sides:
        count = lax.axis_size(axis)
        head = lax.slice_in_dim(cells, 0, width, axis=dim)
        tail = lax.slice_in_dim(cells, cells.shape[dim] - width, cells.shape[dim], axis=dim)
        cells = jnp.concatenate(
            [
                lax.ppermute(tail, axis, [(i, (i + 1) % count) for i in range(count)]),
                cells,
                lax.ppermute(head, axis, [((i + 1) % count, i) for i in range(count)]),
            ],
            axis=dim,
        )
    return cells


def band_diff(padded, axis, count):
    out_shape = list(padded.shape)
    out_shape[axis] = count
    total = jnp.zeros(tuple(out_shape), jnp.float32)
    for shift_k, weight in zip((1, 2, 3), COEFS):
        ahead = lax.slice_in_dim(padded, 3 + shift_k, 3 + shift_k + count, axis=axis)
        behind = lax.slice_in_dim(padded, 3 - shift_k, 3 - shift_k + count, axis=axis)
        total = total + weight * (ahead - behind)
    return total


def span_extend(field, rim_part):
    return jnp.concatenate([rim_part[..., :3], field, rim_part[..., 3:]], axis=-1)


def upper_factor(gram):
    order = gram.shape[0]
    index = jnp.arange(order, dtype=jnp.int32)

    def column_step(j, lower):
        pick = (index == j).astype(gram.dtype)
        row = jnp.dot(pick, lower, precision=lax.Precision.HIGHEST)
        column = jnp.dot(gram, pick, precision=lax.Precision.HIGHEST) - jnp.dot(
            lower, row, precision=lax.Precision.HIGHEST
        )
        pivot = jnp.sqrt(jnp.sum(column * pick))
        below = (index > j).astype(gram.dtype)
        fresh = column * below / pivot + pick * pivot
        return lower + fresh[:, None] * pick[None, :]

    lower = lax.fori_loop(0, order, column_step, jnp.zeros_like(gram))
    return lower.T


def inverse_upper(upper):
    order = upper.shape[0]
    index = jnp.arange(order, dtype=jnp.int32)
    lower = upper.T

    def row_step(j, solved):
        pick = (index == j).astype(upper.dtype)
        row = jnp.dot(pick, lower, precision=lax.Precision.HIGHEST)
        pivot = jnp.sum(row * pick)
        fresh = (pick - jnp.dot(row, solved, precision=lax.Precision.HIGHEST)) / pivot
        return solved + pick[:, None] * fresh[None, :]

    solved = lax.fori_loop(0, order, row_step, jnp.zeros_like(upper))
    return solved.T


def gram_of(matrix):
    return lax.dot_general(
        matrix, matrix, (((0,), (0,)), ((), ())), preferred_element_type=jnp.float32
    )


def local(velocity, span_rim, sketch_old, omega):
    slabs = velocity.shape[2]
    band_rows = velocity.shape[3] - 6
    span_cells = velocity.shape[4]
    extended = extended_2(velocity, (("gx", 2),), 3)
    v_ext = extended[:, 1, :, 3 : 3 + band_rows]
    w_ext = extended[:, 2, :, 3 : 3 + band_rows]
    band = velocity[:, :, :, 3 : 3 + band_rows]
    u_span = span_extend(band[:, 0], span_rim[:, 0])
    v_span = span_extend(band[:, 1], span_rim[:, 1])
    vort_x = band_diff(velocity[:, 2], 2, band_rows) - band_diff(v_span, 3, span_cells)
    vort_y = band_diff(u_span, 3, span_cells) - band_diff(w_ext, 1, slabs)
    vort_z = band_diff(v_ext, 1, slabs) - band_diff(velocity[:, 0], 2, band_rows)
    vort = jnp.stack([vort_x, vort_y, vort_z], axis=1)
    sketch = sketch_old.astype(jnp.float32)
    for snap in range(vort.shape[0]):
        sketch = sketch + vort[snap][..., None] * omega[snap]
    sketch = sketch.astype(jnp.bfloat16)
    matrix = sketch.reshape(-1, sketch.shape[-1])
    total = jnp.float32(matrix.shape[0] * lax.axis_size("gx"))
    local_gram = gram_of(matrix) / total
    factor = upper_factor(lax.psum(local_gram, "gx"))
    inverse_one = inverse_upper(factor).astype(jnp.bfloat16)
    basis = jnp.dot(matrix, inverse_one, preferred_element_type=jnp.float32).astype(jnp.bfloat16)
    return (basis.reshape(sketch.shape), factor)


def solution(mesh):
    in_specs = (
        P(None, None, ("rec", "gx"), None, None),
        P(None, None, ("rec", "gx"), None, None),
        P(None, ("rec", "gx"), None, None, None),
        P(),
    )
    out_specs = (P(None, ("rec", "gx"), None, None, None), P("rec", None))
    return jax.shard_map(local, mesh=mesh, in_specs=in_specs, out_specs=out_specs, check_vma=False)
```

profile of v0, /device:TPU:1, one launch (start us, length us, event | category | flops | bytes accessed | tf_op | source)
XLA Modules:
  0.0 1443.7 jit_solution(5448559899833227195)
XLA Ops:
  7.3 2.6 collective-permute-start
  14.8 2.3 collective-permute-done
  18.7 7.5 add_convert_fusion
  26.3 2.5 copy-done
  28.8 2.4 fusion.21
  31.3 91.8 %all-reduce.2.cloned.1.call-done = f32[256,256]{1,0:T(8,128)} async-done(((f32[256,256]{1,0:T(8,128)}), f32[256,256]{1,0:T(8,128)}) %all-reduce.2.cloned.1.call-update) | async-done | bytes 262160 | tf_op jit(solution)/shard_map/psum | solution.py:102
  123.1 829.0 %while.30 = (s32[]{:T(128)}, f32[256,256]{1,0:T(8,128)S(1)}, f32[256,256]{1,0:T(8,128)}, s32[]{:T(128)}, s32[]{:T(128)}) while((s32[]{:T(128)}, f32[256,256]{1,0:T(8,128)S(1)}, f32[256,256]{1,0:T(8,128)}, s32[]{:T(128)}, s32[]{:T(128)}) %tuple.85), condition=%wide.region_3.0_spmd.clone.clone, body=%wide.region_1.0_spmd.clone.clone.sunk | while | flops 2690306 | bytes 1324397 | solution.py:55
  139.5 1.2 fusion.114
  142.7 1.2 fusion.114
  146.0 1.2 fusion.114
  149.2 1.2 fusion.114
  152.4 1.2 fusion.114
  155.7 1.2 fusion.114
  158.9 1.2 fusion.114
  162.1 1.2 fusion.114
  165.4 1.2 fusion.114
  168.6 1.2 fusion.114
  171.9 1.2 fusion.114
  175.1 1.2 fusion.114
  178.3 1.2 fusion.114
  181.6 1.2 fusion.114
  184.8 1.2 fusion.114
  201.0 1.2 fusion.114
  204.2 1.2 fusion.114
  207.5 1.2 fusion.114
  210.7 1.2 fusion.114
  214.0 1.2 fusion.114
  217.2 1.2 fusion.114
  220.4 1.2 fusion.114
  223.7 1.2 fusion.114
  226.9 1.2 fusion.114
  230.1 1.2 fusion.114
  233.4 1.2 fusion.114
  236.6 1.2 fusion.114
  239.9 1.2 fusion.114
  243.1 1.2 fusion.114
  246.3 1.2 fusion.114
  262.5 1.2 fusion.114
  265.8 1.2 fusion.114
  269.0 1.2 fusion.114
  272.2 1.2 fusion.114
  275.5 1.2 fusion.114
  278.7 1.2 fusion.114
  282.0 1.2 fusion.114
  285.2 1.2 fusion.114
  288.4 1.2 fusion.114
  952.9 476.9 %while.29 = (s32[]{:T(128)}, f32[256,256]{1,0:T(8,128)S(1)}, f32[256,256]{1,0:T(8,128)S(1)}, s32[]{:T(128)}, s32[]{:T(128)}) while((s32[]{:T(128)}, f32[256,256]{1,0:T(8,128)S(1)}, f32[256,256]{1,0:T(8,128)S(1)}, s32[]{:T(128)}, s32[]{:T(128)}) %tuple.88), condition=%wide.region_6.0_spmd.clone, body=%wide.region_4.0_spmd.clone.sunk | while | flops 1837314 | bytes 1058916 | solution.py:71
  1429.9 7.0 convolution_convert_fusion
  (3831 shorter events, 1066.7 us)
Async XLA Ops:
  7.2 115.9 %all-reduce.2.cloned.1.call-start = ((), (), s32[]{:S(2)}) async-start(), calls=%async_computation | async-start | bytes 524288 | tf_op jit(solution)/shard_map/psum | solution.py:102
  7.2 10.9 collective-permute-start.1
  7.3 9.8 collective-permute-start
  14.8 3.9 copy-start.1
  26.3 2.5 copy-start
Sparse Core Ops, SparseCore 0:
  31.4 91.6 all-reduce.1
where the time goes:
time: 1470 us; the launch traced here: 1440 us
  other arithmetic  573 us (39%)
  matrix products  547 us (37%)
  loops' own time  201 us (14%)
  waiting for transfers between devices  94.1 us (6%)
    dot_general x256, matrix products, column_step(): jnp.dot(gram, pick, precision=lax.Precision.HIGHEST)  301 us
    another operation x1, loops' own time, upper_factor(): lower = lax.fori_loop(0, order, column_step, jnp.zeros_like(gram))  189 us
    div x256, other arithmetic, row_step(): (pick - jnp.dot(row, solved, precision=lax.Precision.HIGHEST)) / pivot  170 us
    reduce_sum x256, other arithmetic, column_step(): pivot = jnp.sqrt(jnp.sum(column * pick))  170 us
    reduce_sum x256, other arithmetic, row_step(): pivot = jnp.sum(row * pick)  162 us
    psum x1, waiting for transfers between devices, local(): factor = upper_factor(lax.psum(local_gram, 'gx'))  91.8 us
    dot_general x256, matrix products, column_step(): jnp.dot(lower, row, precision=lax.Precision.HIGHEST)  81.5 us
    dot_general x256, matrix products, column_step(): row = jnp.dot(pick, lower, precision=lax.Precision.HIGHEST)  53.6 us
  transfers between devices with their start and end apart: 3, of which 2 were waited for; matrix products, arithmetic and copies ran while one was open for 0% of the time, Pallas kernels for 0%

commit v1 on v0

--- a/solution.py
+++ b/solution.py
@@ -99,7 +99,11 @@
     matrix = sketch.reshape(-1, sketch.shape[-1])
     total = jnp.float32(matrix.shape[0] * lax.axis_size("gx"))
     local_gram = gram_of(matrix) / total
-    factor = upper_factor(lax.psum(local_gram, "gx"))
+
+    def save_face(in_array, axis_tag):
+        return jnp.sum(jax.lax.all_gather(in_array, axis_tag), axis=0)
+
+    factor = upper_factor(save_face(local_gram, "gx"))
     inverse_one = inverse_upper(factor).astype(jnp.bfloat16)
     basis = jnp.dot(matrix, inverse_one, preferred_element_type=jnp.float32).astype(jnp.bfloat16)
     return (basis.reshape(sketch.shape), factor)

time: 1470 us -> 1190 us (0.81)
  matrix products: 547 us -> 304 us
  waiting for transfers between devices: 94.1 us -> 55.5 us
    dot_general x256, matrix products: 301 us -> 57.9 us  [column_step(): jnp.dot(gram, pick, precision=lax.Precision.HIGHEST)]
    psum x1 -> x0, waiting for transfers between devices: 91.8 us -> none  [local(): factor = upper_factor(lax.psum(local_gram, 'gx'))]
    all_gather x0 -> x1, waiting for transfers between devices: none -> 53.2 us  [save_face(): return jnp.sum(jax.lax.all_gather(in_array, axis_tag), axis=0)]
  transfers between devices with their start and end apart: 3 -> 3, of which waited for: 2 -> 2; matrix products, arithmetic and copies ran while one was open for 0% -> 1% of each run, Pallas kernels for 0% -> 0%
where the time goes in v1:
time: 1190 us; the launch traced here: 1160 us
  other arithmetic  575 us (48%)
  matrix products  304 us (26%)
  loops' own time  201 us (17%)
  waiting for transfers between devices  55.5 us (5%)
  between operations  14.2 us (1%)
  local copies, waits for them, and re-layouts  12.5 us (1%)
    another operation x1, loops' own time, upper_factor(): lower = lax.fori_loop(0, order, column_step, jnp.zeros_like(gram))  189 us
    div x256, other arithmetic, row_step(): (pick - jnp.dot(row, solved, precision=lax.Precision.HIGHEST)) / pivot  170 us
    reduce_sum x256, other arithmetic, column_step(): pivot = jnp.sqrt(jnp.sum(column * pick))  170 us
    reduce_sum x256, other arithmetic, row_step(): pivot = jnp.sum(row * pick)  162 us
    dot_general x256, matrix products, column_step(): jnp.dot(lower, row, precision=lax.Precision.HIGHEST)  81.5 us
    dot_general x256, matrix products, column_step(): jnp.dot(gram, pick, precision=lax.Precision.HIGHEST)  57.9 us
    dot_general x256, matrix products, column_step(): row = jnp.dot(pick, lower, precision=lax.Precision.HIGHEST)  53.6 us
    all_gather x1, waiting for transfers between devices, save_face(): return jnp.sum(jax.lax.all_gather(in_array, axis_tag), axis=0)  53.2 us
  transfers between devices with their start and end apart: 3, of which 2 were waited for; matrix products, arithmetic and copies ran while one was open for 1% of the time, Pallas kernels for 0%

profile of v1, /device:TPU:1, one launch (start us, length us, event | category | flops | bytes accessed | tf_op | source)
XLA Modules:
  0.0 1164.5 jit_solution(17872321920813216173)
XLA Ops:
  7.3 2.6 collective-permute-start
  9.9 1.0 slice_bitcast_fusion.5
  10.9 1.0 slice_bitcast_fusion.4
  11.9 1.0 fusion.73
  13.6 0.8 fusion.76
  14.8 2.3 collective-permute-done
  17.1 1.0 constant_dynamic-update-slice_fusion.1
  18.7 7.5 add_convert_fusion
  26.3 2.5 copy-done
  28.8 2.4 fusion.21
  31.3 53.2 %all-gather.3.cloned.1.call-done = f32[4096,256]{1,0:T(8,128)} async-done(((f32[256,256]{1,0:T(8,128)}), f32[4096,256]{1,0:T(8,128)}) %all-gather.3.cloned.1.call-update) | async-done | bytes 4194320 | tf_op jit(solution)/shard_map/all_gather | solution.py:104
  84.5 2.5 reduce_sum.35
  87.0 585.8 %while.30 = (s32[]{:T(128)}, f32[256,256]{1,0:T(8,128)S(1)}, f32[256,256]{1,0:T(8,128)S(1)}, s32[]{:T(128)}, s32[]{:T(128)}) while((s32[]{:T(128)}, f32[256,256]{1,0:T(8,128)S(1)}, f32[256,256]{1,0:T(8,128)S(1)}, s32[]{:T(128)}, s32[]{:T(128)}) %tuple.85), condition=%wide.region_3.0_spmd.clone.clone, body=%wide.region_1.0_spmd.clone.clone.sunk | while | flops 2690306 | bytes 1324397 | solution.py:55
  672.8 0.8 copy.29
  673.7 476.9 %while.29 = (s32[]{:T(128)}, f32[256,256]{1,0:T(8,128)S(1)}, f32[256,256]{1,0:T(8,128)S(1)}, s32[]{:T(128)}, s32[]{:T(128)}) while((s32[]{:T(128)}, f32[256,256]{1,0:T(8,128)S(1)}, f32[256,256]{1,0:T(8,128)S(1)}, s32[]{:T(128)}, s32[]{:T(128)}) %tuple.88), condition=%wide.region_6.0_spmd.clone, body=%wide.region_4.0_spmd.clone.sunk | while | flops 1837314 | bytes 1058916 | solution.py:71
  674.7 0.7 subtract_divide_fusion.2
  676.6 0.7 subtract_divide_fusion.2
  678.5 0.7 subtract_divide_fusion.2
  680.3 0.7 subtract_divide_fusion.2
  682.2 0.7 subtract_divide_fusion.2
  684.0 0.7 subtract_divide_fusion.2
  685.9 0.7 subtract_divide_fusion.2
  691.5 0.7 subtract_divide_fusion.2
  693.4 0.7 subtract_divide_fusion.2
  695.2 0.7 subtract_divide_fusion.2
  697.1 0.7 subtract_divide_fusion.2
  698.9 0.7 subtract_divide_fusion.2
  700.8 0.7 subtract_divide_fusion.2
  702.7 0.7 subtract_divide_fusion.2
  704.5 0.7 subtract_divide_fusion.2
  708.3 0.7 subtract_divide_fusion.2
  710.1 0.7 subtract_divide_fusion.2
  712.0 0.7 subtract_divide_fusion.2
  713.9 0.7 subtract_divide_fusion.2
  715.7 0.7 subtract_divide_fusion.2
  717.6 0.7 subtract_divide_fusion.2
  719.4 0.7 subtract_divide_fusion.2
  721.3 0.7 subtract_divide_fusion.2
  726.9 0.7 subtract_divide_fusion.2
  728.8 0.7 subtract_divide_fusion.2
  730.6 0.7 subtract_divide_fusion.2
  732.5 0.7 subtract_divide_fusion.2
  734.3 0.7 subtract_divide_fusion.2
  736.2 0.7 subtract_divide_fusion.2
  738.1 0.7 subtract_divide_fusion.2
  739.9 0.7 subtract_divide_fusion.2
  743.7 0.7 subtract_divide_fusion.2
  1150.6 7.0 convolution_convert_fusion
  (3832 shorter events, 842.4 us)
Async XLA Ops:
  7.2 77.4 %all-gather.3.cloned.1.call-start = ((), (), s32[]{:S(2)}) async-start(), calls=%async_computation | async-start | bytes 4456448 | tf_op jit(solution)/shard_map/all_gather | solution.py:104
  7.2 10.9 collective-permute-start.1
  7.3 9.8 collective-permute-start
  14.8 3.9 copy-start.1
  26.3 2.5 copy-start
Sparse Core Ops, SparseCore 0:
  31.4 53.0 all-gather.2
